TPU v7x, 256 devices: a whole 4x4x8 slice. The times are simulated.
256 devices in a mesh: dp: 16 (over z, core), mp: 16 (over y, x).
Axes of the slice: x: 4, y: 4, z: 8, core: 2. Of those that a mesh axis runs over, the one named last changes fastest.
Arguments:
- activations: bfloat16 [16, 1024, 4096], P('dp'), may hold values from -6 to 6
- out_grads: bfloat16 [16, 1024, 8192], P('dp', None, 'mp'), may hold values from -0.1875 to 0.1875
- error_fb: bfloat16 [16, 4096, 8192], P('dp', None, 'mp'), may hold values from -6 to 6
- q_prev: float32 [8192, 128], P('mp'), may hold values from -0.0625 to 0.0625
Outputs:
- new_error: bfloat16 [16, 4096, 8192], P('dp', None, 'mp')
- q_new: float32 [8192, 128], P('mp')
All inputs are finite; a program needn't handle non-finite values.
Results may differ from a plain program's by a relative error of at most 0.001.
Values sent between devices are 32-bit elements; how exact they have to be, the bound alone decides.
A program may use at most 128 MiB of HBM per device.

v0:
```python
import jax
import jax.numpy as jnp
from jax import lax
from jax.sharding import PartitionSpec as P


def orthonormal(p_part, gram):
    chol = jnp.linalg.cholesky(gram)
    return lax.linalg.triangular_solve(chol, p_part, left_side=False, lower=True, transpose_a=True)


def self_gram(p_part):
    return jnp.dot(p_part.T, p_part, precision=lax.Precision.HIGHEST)


def per_device(activations, out_grads, error_fb, q_prev):
    grad_full = lax.dot_general(
        activations[0], out_grads[0], (((0,), (0,)), ((), ())), preferred_element_type=jnp.float32
    )
    merged = grad_full + error_fb[0].astype(jnp.float32)
    p_local = jnp.dot(merged, q_prev, precision=lax.Precision.HIGHEST)
    p_sum = lax.psum(p_local, ("dp", "mp"))
    p_hat = orthonormal(p_sum, self_gram(p_sum))
    q_local = lax.dot_general(
        merged, p_hat, (((0,), (0,)), ((), ())), precision=lax.Precision.HIGHEST
    )
    q_new = lax.psum(q_local, "dp") / lax.axis_size("dp")
    approx = jnp.dot(p_hat, q_new.T, precision=lax.Precision.HIGHEST)
    new_error = (merged - approx).astype(jnp.bfloat16)[None]
    return (new_error, q_new)


def solution(mesh):
    placed = (P("dp", None, None), P("dp", None, "mp"), P("dp", None, "mp"), P("mp", None))
    return jax.shard_map(
        per_device,
        mesh=mesh,
        in_specs=placed,
        out_specs=(P("dp", None, "mp"), P("mp", None)),
        check_vma=False,
    )
```

profile of v0, /device:TPU:1, one launch (start us, length us, event | category | flops | bytes accessed | tf_op | source)
XLA Modules:
  0.0 475.6 jit_solution(18077918757856505209)
XLA Ops:
  7.2 0.0 copy-start
  7.2 0.0 copy-start.5
  7.2 0.0 all-reduce.3.cloned.1.call-start
  7.2 1.2 copy-done
  8.4 12.1 %convert_add_fusion = f32[4096,512]{1,0:T(8,128)S(1)} fusion(bf16[1,1024,4096]{2,1,0:T(8,128)(2,1)} %param.4, bf16[1,4096,512]{2,1,0:T(8,128)(2,1)} %param.6, bf16[1,1024,512]{2,1,0:T(8,128)(2,1)S(1)} %copy-done), kind=kOutput, calls=%fused_computation | convolution fusion | flops 4299161600 | bytes 22020096 | tf_op jit(solution)/shard_map/dot_general | solution.py:17
  20.5 0.0 copy-start.1
  20.6 3.2 copy-done.1
  23.8 0.0 copy-done.5
  23.8 8.1 %fusion.10 = f32[4096,128]{1,0:T(8,128)} fusion(f32[4096,512]{1,0:T(8,128)S(1)} %convert_add_fusion, f32[512,128]{1,0:T(8,128)S(1)} %copy-done.5), kind=kOutput, calls=%fused_computation.17 | convolution fusion | flops 3221225472 | bytes 10747904 | tf_op jit(solution)/shard_map/dot_general | solution.py:21
  31.8 0.0 all-reduce.3.cloned.1.call-update
  31.9 0.2 all-reduce.5.cloned.1.call-start
  32.1 265.9 %all-reduce.3.cloned.1.call-done = f32[4096,128]{1,0:T(8,128)} async-done(((f32[4096,128]{1,0:T(8,128)}), f32[4096,128]{1,0:T(8,128)}) %all-reduce.3.cloned.1.call-update) | async-done | bytes 2097168 | tf_op jit(solution)/shard_map/psum | solution.py:22
  298.0 0.0 copy-start.2
  298.0 5.8 %fusion.11 = f32[128,128]{1,0:T(8,128)S(1)} fusion(f32[4096,128]{1,0:T(8,128)} %all-reduce.3.cloned.1.call-done), kind=kOutput, calls=%fused_computation.18 | convolution fusion | flops 805306368 | bytes 2162688 | tf_op jit(solution)/shard_map/dot_general | solution.py:13
  303.8 0.1 copy.6
  303.9 11.7 %cholesky.16 = f32[128,128]{1,0:T(8,128)S(1)} custom-call(f32[128,128]{1,0:T(8,128)S(1)} %fusion.9), custom_call_target="Cholesky" | custom-call | tf_op jit(solution)/shard_map/jit(cholesky)/cholesky | solution.py:8
  315.7 0.6 compare_reduce_fusion
  316.3 0.7 fusion.6
  317.0 9.8 %custom-call.6 = f32[1,128,128]{1,2,0:T(8,128)S(1)} custom-call(f32[1,128,128]{2,1,0:T(8,128)S(1)} %fusion.6), custom_call_target="InvertDiagBlocksLowerTriangular" | custom-call | tf_op jit(solution)/shard_map/triangular_solve | solution.py:9
  326.8 0.0 copy-done.2
  326.8 1.8 fusion.7
  328.6 0.0 copy-start.3
  328.6 1.4 copy-done.3
  330.0 16.2 %fusion.12 = f32[512,128]{1,0:T(8,128)} fusion(f32[4096,512]{1,0:T(8,128)} %copy-done.1, f32[4096,128]{1,0:T(8,128)S(1)} %fusion.7), kind=kOutput, calls=%fused_computation.19 | convolution fusion | flops 3221225472 | bytes 10747904 | tf_op jit(solution)/shard_map/dot_general | solution.py:24
  346.1 0.0 all-reduce.5.cloned.1.call-update
  346.2 110.5 %all-reduce.5.cloned.1.call-done = f32[512,128]{1,0:T(8,128)} async-done(((f32[512,128]{1,0:T(8,128)}), f32[512,128]{1,0:T(8,128)}) %all-reduce.5.cloned.1.call-update) | async-done | bytes 262160 | tf_op jit(solution)/shard_map/psum | solution.py:27
  456.7 1.0 broadcast_multiply_fusion
  457.6 0.0 copy-start.4
  457.7 11.2 %fusion.4 = bf16[1,4096,512]{2,1,0:T(8,128)(2,1)} fusion(f32[4096,512]{1,0:T(8,128)} %copy-done.1, f32[4096,128]{1,0:T(8,128)} %copy-done.3, f32[512,128]{1,0:T(8,128)S(1)} %broadcast_multiply_fusion), kind=kOutput, calls=%fused_computation.4 | convolution fusion | flops 3225419776 | bytes 14942208 | tf_op jit(solution)/shard_map/dot_general | solution.py:28
  468.8 0.0 copy-done.4
  (2 shorter events, 0.0 us)
Async XLA Ops:
  7.2 1.2 copy-start
  7.2 16.6 %copy-start.5 = (f32[512,128]{1,0:T(8,128)S(1)}, f32[512,128]{1,0:T(8,128)}, u32[]{:S(2)}) copy-start(f32[512,128]{1,0:T(8,128)} %param.7) | copy-start | bytes 786436
  7.2 290.8 %all-reduce.3.cloned.1.call-start = ((), (), s32[]{:S(2)}) async-start(), calls=%async_computation | async-start | bytes 4194304 | tf_op jit(solution)/shard_map/psum | solution.py:22
  20.5 3.2 copy-start.1
  31.9 424.8 %all-reduce.5.cloned.1.call-start = ((), (), s32[]{:S(2)}) async-start(), calls=%async_computation.1 | async-start | bytes 524288 | tf_op jit(solution)/shard_map/psum | solution.py:27
  298.0 28.8 %copy-start.2 = (f32[4096,128]{1,0:T(8,128)S(1)}, f32[4096,128]{1,0:T(8,128)}, u32[]{:S(2)}) copy-start(f32[4096,128]{1,0:T(8,128)} %all-reduce.3.cloned.1.call-done) | copy-start | bytes 6291460
  328.6 1.4 copy-start.3
  457.6 11.2 %copy-start.4 = (f32[512,128]{1,0:T(8,128)}, f32[512,128]{1,0:T(8,128)S(1)}, u32[]{:S(2)}) copy-start(f32[512,128]{1,0:T(8,128)S(1)} %broadcast_multiply_fusion) | copy-start | bytes 786436
Sparse Core Ops, SparseCore 0:
  32.0 265.9 all-reduce.2
  346.3 110.3 all-reduce.4
where the time goes:
time: 476 us
  waiting for transfers between devices  376 us (79%)
  matrix products  55.1 us (12%)
  other arithmetic  23.8 us (5%)
  between operations  14.1 us (3%)
  local copies, waits for them, and re-layouts  5.86 us (1%)
    psum x1, waiting for transfers between devices, per_device(): p_sum = lax.psum(p_local, ('dp', 'mp'))  266 us
    psum x1, waiting for transfers between devices, per_device(): q_new = lax.psum(q_local, 'dp') / lax.axis_size('dp')  111 us
    dot_general x1, matrix products, per_device(): lax.dot_general(merged, p_hat, (((0,), (0,)), ((), ())), precision=lax.Pr...  16.2 us
    another operation x3, other arithmetic, orthonormal(): chol = jnp.linalg.cholesky(gram)  12.4 us
    dot_general x1, matrix products, per_device(): lax.dot_general(activations[0], out_grads[0], (((0,), (0,)), ((), ())), p...  12.1 us
    dot_general x1, matrix products, per_device(): approx = jnp.dot(p_hat, q_new.T, precision=lax.Precision.HIGHEST)  11.2 us
    another operation x2, other arithmetic, orthonormal(): lax.linalg.triangular_solve(chol, p_part, left_side=False, lower=True, tr...  10.5 us
  transfers between devices with their start and end apart: 2, of which 2 were waited for; matrix products, arithmetic and copies ran while one was open for 0% of the time, Pallas kernels for 0%

commit v1 on v0

--- a/solution.py
+++ b/solution.py
@@ -19,7 +19,7 @@
     )
     merged = grad_full + error_fb[0].astype(jnp.float32)
     p_local = jnp.dot(merged, q_prev, precision=lax.Precision.HIGHEST)
-    p_sum = lax.psum(p_local, ("dp", "mp"))
+    p_sum = lax.psum(lax.psum(p_local, "mp"), "dp")
     p_hat = orthonormal(p_sum, self_gram(p_sum))
     q_local = lax.dot_general(
         merged, p_hat, (((0,), (0,)), ((), ())), precision=lax.Precision.HIGHEST

time: 476 us -> 432 us (0.908)
  waiting for transfers between devices: 376 us -> 333 us
    psum x1 -> x2, waiting for transfers between devices: 266 us -> 222 us  [per_device(): p_sum = lax.psum(lax.psum(p_local, 'mp'), 'dp')]
  transfers between devices with their start and end apart: 2 -> 3, of which waited for: 2 -> 3; matrix products, arithmetic and copies ran while one was open for 0% -> 0% of each run, Pallas kernels for 0% -> 0%
where the time goes in v1:
time: 432 us
  waiting for transfers between devices  333 us (77%)
  matrix products  55.1 us (13%)
  other arithmetic  23.8 us (6%)
  between operations  13.9 us (3%)
  local copies, waits for them, and re-layouts  5.86 us (1%)
    psum x2, waiting for transfers between devices, per_device(): p_sum = lax.psum(lax.psum(p_local, 'mp'), 'dp')  222 us
    psum x1, waiting for transfers between devices, per_device(): q_new = lax.psum(q_local, 'dp') / lax.axis_size('dp')  111 us
    dot_general x1, matrix products, per_device(): lax.dot_general(merged, p_hat, (((0,), (0,)), ((), ())), precision=lax.Pr...  16.2 us
    another operation x3, other arithmetic, orthonormal(): chol = jnp.linalg.cholesky(gram)  12.4 us
    dot_general x1, matrix products, per_device(): lax.dot_general(activations[0], out_grads[0], (((0,), (0,)), ((), ())), p...  12.1 us
    dot_general x1, matrix products, per_device(): approx = jnp.dot(p_hat, q_new.T, precision=lax.Precision.HIGHEST)  11.1 us
    another operation x2, other arithmetic, orthonormal(): lax.linalg.triangular_solve(chol, p_part, left_side=False, lower=True, tr...  10.5 us
  transfers between devices with their start and end apart: 3, of which 3 were waited for; matrix products, arithmetic and copies ran while one was open for 0% of the time, Pallas kernels for 0%

profile of v1, /device:TPU:1, one launch (start us, length us, event | category | flops | bytes accessed | tf_op | source)
XLA Modules:
  0.0 431.6 jit_solution(10779407103708706681)
XLA Ops:
  7.2 0.0 copy-start
  7.2 0.0 copy-start.5
  7.2 0.0 all-reduce.4.cloned.1.call-start
  7.2 1.2 copy-done
  8.4 12.1 %convert_add_fusion = f32[4096,512]{1,0:T(8,128)S(1)} fusion(bf16[1,1024,4096]{2,1,0:T(8,128)(2,1)} %param.4, bf16[1,4096,512]{2,1,0:T(8,128)(2,1)} %param.6, bf16[1,1024,512]{2,1,0:T(8,128)(2,1)S(1)} %copy-done), kind=kOutput, calls=%fused_computation | convolution fusion | flops 4299161600 | bytes 22020096 | tf_op jit(solution)/shard_map/dot_general | solution.py:17
  20.5 0.0 copy-start.1
  20.6 3.2 copy-done.1
  23.8 0.0 copy-done.5
  23.8 8.1 %fusion.10 = f32[4096,128]{1,0:T(8,128)} fusion(f32[4096,512]{1,0:T(8,128)S(1)} %convert_add_fusion, f32[512,128]{1,0:T(8,128)S(1)} %copy-done.5), kind=kOutput, calls=%fused_computation.17 | convolution fusion | flops 3221225472 | bytes 10747904 | tf_op jit(solution)/shard_map/dot_general | solution.py:21
  31.8 0.0 all-reduce.4.cloned.1.call-update
  31.9 0.0 all-reduce.6.cloned.1.call-start
  31.9 103.7 %all-reduce.4.cloned.1.call-done = f32[4096,128]{1,0:T(8,128)} async-done(((f32[4096,128]{1,0:T(8,128)}), f32[4096,128]{1,0:T(8,128)}) %all-reduce.4.cloned.1.call-update) | async-done | bytes 2097168 | tf_op jit(solution)/shard_map/psum | solution.py:22
  135.6 0.0 all-reduce.6.cloned.1.call-update
  135.6 0.2 all-reduce.8.cloned.1.call-start
  135.8 118.2 %all-reduce.6.cloned.1.call-done = f32[4096,128]{1,0:T(8,128)} async-done(((f32[4096,128]{1,0:T(8,128)}), f32[4096,128]{1,0:T(8,128)}) %all-reduce.6.cloned.1.call-update) | async-done | bytes 2097168 | tf_op jit(solution)/shard_map/psum | solution.py:22
  254.1 5.8 %fusion.11 = f32[128,128]{1,0:T(8,128)S(1)} fusion(f32[4096,128]{1,0:T(8,128)} %all-reduce.6.cloned.1.call-done), kind=kOutput, calls=%fused_computation.18 | convolution fusion | flops 805306368 | bytes 2162688 | tf_op jit(solution)/shard_map/dot_general | solution.py:13
  259.9 0.1 copy.6
  260.0 11.7 %cholesky.16 = f32[128,128]{1,0:T(8,128)S(1)} custom-call(f32[128,128]{1,0:T(8,128)S(1)} %fusion.9), custom_call_target="Cholesky" | custom-call | tf_op jit(solution)/shard_map/jit(cholesky)/cholesky | solution.py:8
  271.7 0.6 compare_reduce_fusion
  272.4 0.7 fusion.6
  273.1 9.8 %custom-call.6 = f32[1,128,128]{1,2,0:T(8,128)S(1)} custom-call(f32[1,128,128]{2,1,0:T(8,128)S(1)} %fusion.6), custom_call_target="InvertDiagBlocksLowerTriangular" | custom-call | tf_op jit(solution)/shard_map/triangular_solve | solution.py:9
  282.9 0.0 copy-done.2
  282.9 1.8 fusion.7
  284.7 0.0 copy-start.3
  284.7 1.4 copy-done.3
  286.1 16.2 %fusion.12 = f32[512,128]{1,0:T(8,128)} fusion(f32[4096,512]{1,0:T(8,128)} %copy-done.1, f32[4096,128]{1,0:T(8,128)S(1)} %fusion.7), kind=kOutput, calls=%fused_computation.19 | convolution fusion | flops 3221225472 | bytes 10747904 | tf_op jit(solution)/shard_map/dot_general | solution.py:24
  302.2 0.0 all-reduce.8.cloned.1.call-update
  302.2 110.6 %all-reduce.8.cloned.1.call-done = f32[512,128]{1,0:T(8,128)} async-done(((f32[512,128]{1,0:T(8,128)}), f32[512,128]{1,0:T(8,128)}) %all-reduce.8.cloned.1.call-update) | async-done | bytes 262160 | tf_op jit(solution)/shard_map/psum | solution.py:27
  412.9 1.0 broadcast_multiply_fusion
  413.9 0.0 copy-start.4
  413.9 11.1 %fusion.4 = bf16[1,4096,512]{2,1,0:T(8,128)(2,1)} fusion(f32[4096,512]{1,0:T(8,128)} %copy-done.1, f32[4096,128]{1,0:T(8,128)} %copy-done.3, f32[512,128]{1,0:T(8,128)S(1)} %broadcast_multiply_fusion), kind=kOutput, calls=%fused_computation.4 | convolution fusion | flops 3225419776 | bytes 14942208 | tf_op jit(solution)/shard_map/dot_general | solution.py:28
  425.0 0.0 copy-done.4
  (3 shorter events, 0.0 us)
Async XLA Ops:
  7.2 1.2 copy-start
  7.2 16.6 %copy-start.5 = (f32[512,128]{1,0:T(8,128)S(1)}, f32[512,128]{1,0:T(8,128)}, u32[]{:S(2)}) copy-start(f32[512,128]{1,0:T(8,128)} %param.7) | copy-start | bytes 786436
  7.2 128.4 %all-reduce.4.cloned.1.call-start = ((), (), s32[]{:S(2)}) async-start(), calls=%async_computation | async-start | bytes 4194304 | tf_op jit(solution)/shard_map/psum | solution.py:22
  20.5 3.2 copy-start.1
  31.9 222.2 %all-reduce.6.cloned.1.call-start = ((), (), s32[]{:S(2)}) async-start(), calls=%async_computation.1 | async-start | bytes 4194304 | tf_op jit(solution)/shard_map/psum | solution.py:22
  135.6 277.3 %all-reduce.8.cloned.1.call-start = ((), (), s32[]{:S(2)}) async-start(), calls=%async_computation.2 | async-start | bytes 524288 | tf_op jit(solution)/shard_map/psum | solution.py:27
  254.1 28.8 %copy-start.2 = (f32[4096,128]{1,0:T(8,128)S(1)}, f32[4096,128]{1,0:T(8,128)}, u32[]{:S(2)}) copy-start(f32[4096,128]{1,0:T(8,128)} %all-reduce.6.cloned.1.call-done) | copy-start | bytes 6291460
  284.7 1.4 copy-start.3
  413.9 11.2 %copy-start.4 = (f32[512,128]{1,0:T(8,128)}, f32[512,128]{1,0:T(8,128)S(1)}, u32[]{:S(2)}) copy-start(f32[512,128]{1,0:T(8,128)S(1)} %broadcast_multiply_fusion) | copy-start | bytes 786436
Sparse Core Ops, SparseCore 0:
  32.0 103.5 all-reduce.3
  137.9 116.0 all-reduce.5
  302.4 110.4 all-reduce.7
